TPU v7x, 32 devices: a whole 2x2x4 slice. The times are simulated.
32 devices in a mesh: grp: 2 (over x), wide: 16 (over z, y, core).
Axes of the slice: x: 2, y: 2, z: 4, core: 2. Of those that a mesh axis runs over, the one named last changes fastest.
Arguments:
- queries: bfloat16 [256, 4096], P(('grp', 'wide')), parts along dimension 0, may hold values from -8 to 8
- draft_keys: bfloat16 [256, 512], P(('grp', 'wide')), parts along dimension 0, may hold values from -8 to 8
- draft_values: bfloat16 [256, 512], P(('grp', 'wide')), parts along dimension 0, may hold values from -24 to 24
- cache_keys: bfloat16 [262144, 128], P(('grp', 'wide')), parts along dimension 0, may hold values from -8 to 8
- cache_values: bfloat16 [262144, 128], P(('grp', 'wide')), parts along dimension 0, may hold values from -24 to 24
- block_owner: int32 [32], P('grp'), parts along dimension 0, may hold values from 0 to 15, each once
- block_lengths: int32 [32], P('grp'), parts along dimension 0, may hold values from 1024 to 8192, as said below
- draft_mask: int32 [4, 64, 64], P('grp'), parts along dimension 0, may hold values from 0 to 1, as said below
- out_weight: bfloat16 [4096, 8192], P(None, 'wide'), may hold values from -1 to 1
- norm_gain: float32 [8192], replicated, may hold values from 0.25 to 1.75
- gate_weight: bfloat16 [8192, 14336], P(None, 'wide'), may hold values from -0.0625 to 0.0625
- up_weight: bfloat16 [8192, 14336], P(None, 'wide'), may hold values from -0.0625 to 0.0625
Outputs:
- projected: bfloat16 [256, 8192], P('grp', 'wide'), parts along dimension 0
- hidden: bfloat16 [256, 14336], P('grp', 'wide'), parts along dimension 0
There are 2 independent parts, one for each index of `grp`. A program takes and returns all parts, laid end to end along the dimension named above; an argument that names none is the same for every part. Nothing has to cross between parts.
Inputs may be any that keep to these rules, and one draw needn't show every extreme that they name: `block_owner`: each device holds exactly one block. `block_lengths`: at most 8192 rows a block, and some block has exactly 8192 rows. In each sequence row 0 is the root of a tree in which every other row's parent lies 1 to 4 rows before it; draft_mask[s, i, t] is 1 exactly when t is i or an ancestor of i.
All inputs are finite; a program needn't handle non-finite values.
Results may differ from a plain program's by a relative error of at most 0.02.
Values may be sent and summed in bfloat16 or wider, within the bound.
A program may use at most 128 MiB of HBM per device.

v0:
```python
import math
import jax
import jax.numpy as jnp
from jax import lax
from jax.sharding import PartitionSpec as P

very_low = -1e30
epsilon = 1e-05


def block_update(state, query_rows, block_keys, block_values, valid, scale):
    running, total, weighted = state
    scores = (
        jnp.einsum("igc,kc->igk", query_rows, block_keys, preferred_element_type=jnp.float32)
        * scale
    )
    scores = jnp.where(valid, scores, very_low)
    newest = jnp.maximum(running, jnp.max(scores, axis=-1))
    factor = jnp.exp(running - newest)
    weights = jnp.where(valid, jnp.exp(scores - newest[..., None]), 0.0)
    total = total * factor + jnp.sum(weights, axis=-1)
    weighted = weighted * factor[..., None] + jnp.einsum(
        "igk,kc->igc",
        weights.astype(jnp.bfloat16),
        block_values,
        preferred_element_type=jnp.float32,
    )
    return (newest, total, weighted)


def attend(query_rows, keys, values, length, own_keys, own_values, own_valid):
    block_size = min(512, keys.shape[0])
    scale = 1.0 / math.sqrt(query_rows.shape[2])
    rows_count = query_rows.shape[0]
    heads = query_rows.shape[1]
    state = (
        jnp.full((rows_count, heads), very_low, jnp.float32),
        jnp.zeros((rows_count, heads), jnp.float32),
        jnp.zeros((rows_count, heads, query_rows.shape[2]), jnp.float32),
    )
    offsets = jnp.arange(block_size, dtype=jnp.int32)

    def advance(number, carry):
        begin = (number * block_size).astype(jnp.int32)
        block_keys = lax.dynamic_slice_in_dim(keys, begin, block_size, 0)
        block_values = lax.dynamic_slice_in_dim(values, begin, block_size, 0)
        valid = (begin + offsets < length)[None, None, :]
        return block_update(carry, query_rows, block_keys, block_values, valid, scale)

    count = (length + block_size - 1) // block_size
    state = lax.fori_loop(jnp.int32(0), count, advance, state)
    return block_update(state, query_rows, own_keys, own_values, own_valid[:, None, :], scale)


def per_device(
    queries,
    draft_keys,
    draft_values,
    cache_keys,
    cache_values,
    block_owner,
    block_lengths,
    draft_mask,
    out_weight,
    norm_gain,
    gate_weight,
    up_weight,
):
    devices = lax.axis_size("wide")
    own_index = lax.axis_index("wide")
    head_size = cache_keys.shape[1]
    key_heads = draft_keys.shape[1] // head_size
    group_width = queries.shape[1] // key_heads
    group = group_width // head_size
    sequences = draft_mask.shape[0]
    draft_rows = draft_mask.shape[1]
    all_rows = sequences * draft_rows
    local_rows = queries.shape[0]
    heads_all = key_heads * group
    blocks_per_pair = devices // (sequences * key_heads)
    device_ids = jnp.arange(devices, dtype=jnp.int32)
    owned = (block_owner[None, :] == device_ids[:, None]).astype(jnp.int32)
    device_block = jnp.sum(owned * device_ids[None, :], axis=1)
    device_pair = device_block // blocks_per_pair
    device_sequence = device_pair // key_heads
    device_head = device_pair % key_heads
    device_length = jnp.sum(owned * block_lengths[None, :], axis=1)
    picker = (device_ids == own_index).astype(jnp.int32)
    own_block = jnp.sum(picker * device_block)
    own_sequence = jnp.sum(picker * device_sequence)
    own_head = jnp.sum(picker * device_head)
    own_length = jnp.sum(picker * device_length)
    is_last = own_block % blocks_per_pair == blocks_per_pair - 1
    row_start = own_sequence * draft_rows
    head_numbers = jnp.arange(key_heads, dtype=jnp.int32)
    every_query, every_key, every_value = (
        lax.all_gather(queries, "wide", axis=0, tiled=True),
        lax.all_gather(draft_keys, "wide", axis=0, tiled=True),
        lax.all_gather(draft_values, "wide", axis=0, tiled=True),
    )
    query_columns = own_head * group_width
    key_columns = own_head * head_size
    pair_queries = lax.dynamic_slice_in_dim(
        lax.dynamic_slice_in_dim(every_query, row_start, draft_rows, 0),
        query_columns,
        group_width,
        1,
    )
    pair_keys = lax.dynamic_slice_in_dim(
        lax.dynamic_slice_in_dim(every_key, row_start, draft_rows, 0), key_columns, head_size, 1
    )
    pair_values = lax.dynamic_slice_in_dim(
        lax.dynamic_slice_in_dim(every_value, row_start, draft_rows, 0), key_columns, head_size, 1
    )
    own_head = jnp.sum(picker * device_head)
    query_rows = pair_queries.reshape(draft_rows, group, head_size)
    own_valid = (
        lax.dynamic_index_in_dim(draft_mask, own_sequence, 0, keepdims=False) > 0
    ) & is_last
    running, total, weighted = attend(
        query_rows, cache_keys, cache_values, own_length, pair_keys, pair_values, own_valid
    )
    block_output = (weighted / total[..., None]).astype(jnp.bfloat16)
    slot_peak = lax.dynamic_update_slice(
        jnp.full((all_rows, group), very_low, jnp.float32), running, (row_start, jnp.int32(0))
    ).reshape(devices, local_rows, group)
    slot_total = lax.dynamic_update_slice(
        jnp.zeros((all_rows, group), jnp.float32), total, (row_start, jnp.int32(0))
    ).reshape(devices, local_rows, group)
    slot_output = lax.dynamic_update_slice(
        jnp.zeros((all_rows, group, head_size), jnp.bfloat16),
        block_output,
        (row_start, jnp.int32(0), jnp.int32(0)),
    ).reshape(devices, local_rows, group, head_size)
    back_peak, back_total = (
        lax.all_to_all(slot_peak, "wide", split_axis=0, concat_axis=0, tiled=True),
        lax.all_to_all(slot_total, "wide", split_axis=0, concat_axis=0, tiled=True),
    )
    back_output = lax.all_to_all(slot_output, "wide", split_axis=0, concat_axis=0, tiled=True)
    member = device_head[:, None] == head_numbers[None, :]
    spread = jnp.where(member[:, None, :, None], back_peak[:, :, None, :], very_low)
    highest = jnp.max(spread, axis=0)
    mixing = jnp.exp(spread - highest[None]) * back_total[:, :, None, :]
    row_total = jnp.sum(mixing, axis=0)
    row_weighted = jnp.einsum(
        "srgj,srjc->rgjc", mixing, back_output.astype(jnp.float32), precision=lax.Precision.HIGHEST
    )
    attended_rows = (
        (row_weighted / row_total[..., None])
        .astype(jnp.bfloat16)
        .reshape(local_rows, heads_all * head_size)
    )
    combined = jnp.dot(
        lax.all_gather(attended_rows, "wide", axis=0, tiled=True),
        out_weight,
        preferred_element_type=jnp.float32,
    )
    projected = combined.astype(jnp.bfloat16)
    columns = projected.shape[1]
    branch = lax.optimization_barrier(projected).astype(jnp.float32)
    squares = lax.psum(jnp.sum(branch * branch, axis=1), "wide")
    inverse = lax.rsqrt(squares / (columns * devices) + epsilon)
    gain_part = lax.dynamic_slice_in_dim(norm_gain, own_index * columns, columns, 0)
    normed = (branch * inverse[:, None] * gain_part[None, :]).astype(jnp.bfloat16)
    piece = lax.all_gather(normed, "wide", axis=1, tiled=True)
    gate = jnp.dot(piece, gate_weight, preferred_element_type=jnp.float32)
    upward = jnp.dot(piece, up_weight, preferred_element_type=jnp.float32)
    hidden = (jax.nn.silu(gate) * upward).astype(jnp.bfloat16)
    return (projected, hidden)


def solution(mesh):
    placed = (
        P(("grp", "wide"), None),
        P(("grp", "wide"), None),
        P(("grp", "wide"), None),
        P(("grp", "wide"), None),
        P(("grp", "wide"), None),
        P("grp"),
        P("grp"),
        P("grp", None, None),
        P(None, "wide"),
        P(),
        P(None, "wide"),
        P(None, "wide"),
    )
    return jax.shard_map(
        per_device,
        mesh=mesh,
        in_specs=placed,
        out_specs=(P("grp", "wide"), P("grp", "wide")),
        check_vma=False,
    )
```

profile of v0, /device:TPU:0, one launch (start us, length us, event | category | flops | bytes accessed | tf_op | source)
XLA Modules:
  0.0 300.9 jit_solution(8862913507777741700)
XLA Ops:
  7.9 0.8 select_reduce_fusion.2
  16.7 23.9 %all_gather.16 = bf16[128,512]{1,0:T(8,128)(2,1)S(1)} all-gather(bf16[8,512]{1,0:T(8,128)(2,1)} %param.15), channel_id=1, replica_groups=mesh['grp'=2,'wide'=16] {'wide'}, dimensions={0}, use_global_device_ids=true | all-gather | bytes 139264 | tf_op jit(solution)/shard_map/all_gather | solution.py:98
  41.4 9.5 %all-gather.4.cloned.1.call-done = bf16[128,4096]{1,0:T(8,128)(2,1)} async-done(((bf16[8,4096]{1,0:T(8,128)(2,1)}), bf16[128,4096]{1,0:T(8,128)(2,1)}) %all-gather.4.cloned.1.call-update) | async-done | bytes 1048592 | tf_op jit(solution)/shard_map/all_gather | solution.py:97
  50.9 1.0 dynamic-slice_bitcast_fusion.1
  52.5 11.5 %while.15 = (s32[]{:T(128)}, f32[64,8]{0,1:T(8,128)S(1)}, f32[64,8]{0,1:T(8,128)S(1)}, f32[64,8,128]{2,1,0:T(8,128)S(1)}, s32[]{:T(128)}, /*index=5*/s32[]{:T(12...) while((s32[]{:T(128)}, f32[64,8]{0,1:T(8,128)S(1)}, ...), condition=%wide.region_8.9_spmd.clone, body=%wide.region_5.8_spmd.clone.sunk | while | flops 136185856 | bytes 4099771 | solution.py:51
  53.3 1.3 fusion.69
  55.0 1.3 convolution_add_fusion.3
  57.1 1.3 fusion.69
  58.9 1.3 convolution_add_fusion.3
  60.9 1.3 fusion.69
  62.7 1.3 convolution_add_fusion.3
  65.5 52.4 %all-to-all-start.2 = ((f32[16,8,8]{1,2,0:T(8,128)}), f32[16,8,8]{1,2,0:T(8,128)S(1)}, u32[]{:S(2)}, u32[]{:S(2)}) async-start(f32[16,8,8]{1,2,0:T(8,128)} %copy.68), calls=%async_computation.2 | async-start | bytes 131072 | tf_op jit(solution)/shard_map/all_to_all | solution.py:137
  117.9 22.1 %all_gather.17 = bf16[128,512]{1,0:T(8,128)(2,1)S(1)} all-gather(bf16[8,512]{1,0:T(8,128)(2,1)S(1)} %copy-done.2), channel_id=1, replica_groups=mesh['grp'=2,'wide'=16] {'wide'}, dimensions={0}, use_global_device_ids=true | all-gather | bytes 139264 | tf_op jit(solution)/shard_map/all_gather | solution.py:99
  141.1 3.5 %all-to-all-start.1 = ((f32[16,8,8]{1,2,0:T(8,128)}), f32[16,8,8]{1,2,0:T(8,128)S(1)}, u32[]{:S(2)}, u32[]{:S(2)}) async-start(f32[16,8,8]{1,2,0:T(8,128)} %copy.66), calls=%async_computation.1 | async-start | bytes 131072 | tf_op jit(solution)/shard_map/all_to_all | solution.py:136
  145.4 0.9 fusion.18
  146.3 5.2 %all-to-all-done.1 = f32[16,8,8]{1,2,0:T(8,128)S(1)} async-done(((f32[16,8,8]{1,2,0:T(8,128)}), f32[16,8,8]{1,2,0:T(8,128)S(1)}, u32[]{:S(2)}, u32[]{:S(2)}) %all-to-all-start.1) | async-done | bytes 4128 | tf_op jit(solution)/shard_map/all_to_all | solution.py:136
  151.5 3.5 %all-to-all-start = ((bf16[16,8,8,128]{3,2,1,0:T(8,128)(2,1)}), bf16[16,8,8,128]{3,2,1,0:T(8,128)(2,1)S(1)}, u32[]{:S(2)}, u32[]{:S(2)}) async-start(bf16[16,8,8,128]{3,2,1,0:T(8,128)(2,1)} %bitcast.3), calls=%async_computation | async-start | bytes 524288 | tf_op jit(solution)/shard_map/all_to_all | solution.py:139
  155.7 9.3 %all-to-all-done = bf16[16,8,8,128]{3,2,1,0:T(8,128)(2,1)S(1)} async-done(((bf16[16,8,8,128]{3,2,1,0:T(8,128)(2,1)}), bf16[16,8,8,128]{3,2,1,0:T(8,128)(2,1)S(1)}, u32[]{:S(2)}, u32[]{:S(2)}) %all-to-all-start) | async-done | bytes 262176 | tf_op jit(solution)/shard_map/all_to_all | solution.py:139
  167.1 36.5 %all-gather.6.cloned.1.call-done = bf16[128,4096]{1,0:T(8,128)(2,1)} async-done(((bf16[8,4096]{1,0:T(8,128)(2,1)}), bf16[128,4096]{1,0:T(8,128)(2,1)}) %all-gather.6.cloned.1.call-update) | async-done | bytes 1048592 | tf_op jit(solution)/shard_map/all_gather | solution.py:154
  203.5 3.2 %convolution_convert_fusion = bf16[128,512]{1,0:T(8,128)(2,1)S(1)} fusion(bf16[128,4096]{1,0:T(8,128)(2,1)} %all-gather.6.cloned.1.call-done, bf16[4096,512]{1,0:T(8,128)(2,1)} %param.22), kind=kOutput, calls=%fused_computation.27 | convolution fusion | flops 536936448 | bytes 5373952 | tf_op jit(solution)/shard_map/dot_general | solution.py:153
  206.9 31.6 %psum.7 = f32[128]{0:T(128)S(1)} all-reduce(f32[128]{0:T(128)S(1)} %fusion.21), channel_id=1, replica_groups=mesh['grp'=2,'wide'=16] {'wide'}, use_global_device_ids=true, to_apply=%region_15.16 | all-reduce | flops 128 | bytes 1024 | tf_op jit(solution)/shard_map/psum | solution.py:161
  239.3 38.4 %all-gather.8.cloned.1.call-done = bf16[128,8192]{1,0:T(8,128)(2,1)} async-done(((bf16[128,512]{1,0:T(8,128)(2,1)}), bf16[128,8192]{1,0:T(8,128)(2,1)}) %all-gather.8.cloned.1.call-update) | async-done | bytes 2097168 | tf_op jit(solution)/shard_map/all_gather | solution.py:165
  277.7 8.3 %fusion.50 = f32[128,896]{1,0:T(8,128)S(1)} fusion(bf16[128,8192]{1,0:T(8,128)(2,1)} %all-gather.8.cloned.1.call-done, bf16[8192,896]{1,0:T(8,128)(2,1)} %param.24), kind=kOutput, calls=%fused_computation.90 | convolution fusion | flops 1879048192 | bytes 17235968 | tf_op jit(solution)/shard_map/dot_general | solution.py:166
  286.1 8.3 %fusion.14 = bf16[128,896]{1,0:T(8,128)(2,1)} fusion(bf16[128,8192]{1,0:T(8,128)(2,1)S(1)} %copy-done, bf16[8192,896]{1,0:T(8,128)(2,1)} %param.25, f32[128,896]{1,0:T(8,128)S(1)} %fusion.50), kind=kOutput, calls=%fused_computation.20 | convolution fusion | flops 1879736320 | bytes 17465344 | tf_op jit(solution)/shard_map/dot_general | solution.py:167
  (69 shorter events, 13.8 us)
Async XLA Ops:
  7.2 43.8 %all-gather.4.cloned.1.call-start = ((), (), s32[]{:S(2)}) async-start(), calls=%async_computation.3 | async-start | bytes 1114112 | tf_op jit(solution)/shard_map/all_gather | solution.py:97
  52.5 65.3 %copy-start.2 = (bf16[8,512]{1,0:T(8,128)(2,1)S(1)}, bf16[8,512]{1,0:T(8,128)(2,1)}, u32[]{:S(2)}) copy-start(bf16[8,512]{1,0:T(8,128)(2,1)} %param.16) | copy-start | bytes 24580
  65.5 75.7 %all-to-all-start.2 = ((f32[16,8,8]{1,2,0:T(8,128)}), f32[16,8,8]{1,2,0:T(8,128)S(1)}, u32[]{:S(2)}, u32[]{:S(2)}) async-start(f32[16,8,8]{1,2,0:T(8,128)} %copy.68), calls=%async_computation.2 | async-start | bytes 131072 | tf_op jit(solution)/shard_map/all_to_all | solution.py:137
  141.1 10.4 %all-to-all-start.1 = ((f32[16,8,8]{1,2,0:T(8,128)}), f32[16,8,8]{1,2,0:T(8,128)S(1)}, u32[]{:S(2)}, u32[]{:S(2)}) async-start(f32[16,8,8]{1,2,0:T(8,128)} %copy.66), calls=%async_computation.1 | async-start | bytes 131072 | tf_op jit(solution)/shard_map/all_to_all | solution.py:136
  151.5 13.5 %all-to-all-start = ((bf16[16,8,8,128]{3,2,1,0:T(8,128)(2,1)}), bf16[16,8,8,128]{3,2,1,0:T(8,128)(2,1)S(1)}, u32[]{:S(2)}, u32[]{:S(2)}) async-start(bf16[16,8,8,128]{3,2,1,0:T(8,128)(2,1)} %bitcast.3), calls=%async_computation | async-start | bytes 524288 | tf_op jit(solution)/shard_map/all_to_all | solution.py:139
  155.0 48.5 %all-gather.6.cloned.1.call-start = ((), (), s32[]{:S(2)}) async-start(), calls=%async_computation.4 | async-start | bytes 1114112 | tf_op jit(solution)/shard_map/all_gather | solution.py:154
  166.3 111.5 %all-gather.8.cloned.1.call-start = ((), (), s32[]{:S(2)}) async-start(), calls=%async_computation.5 | async-start | bytes 2228224 | tf_op jit(solution)/shard_map/all_gather | solution.py:165
  206.8 79.3 %copy-start.1 = (bf16[128,512]{1,0:T(8,128)(2,1)}, bf16[128,512]{1,0:T(8,128)(2,1)S(1)}, u32[]{:S(2)}) copy-start(bf16[128,512]{1,0:T(8,128)(2,1)S(1)} %convolution_convert_fusion) | copy-start | bytes 393220
  277.7 8.3 %copy-start = (bf16[128,8192]{1,0:T(8,128)(2,1)S(1)}, bf16[128,8192]{1,0:T(8,128)(2,1)}, u32[]{:S(2)}) copy-start(bf16[128,8192]{1,0:T(8,128)(2,1)} %all-gather.8.cloned.1.call-done) | copy-start | bytes 6291460
Sparse Core Ops, SparseCore 0:
  10.1 40.7 all-gather.3
  166.4 37.1 all-gather.5
  239.4 38.2 all-gather.7
where the time goes:
time: 302 us; the launch traced here: 301 us
  waiting for transfers between devices  99.6 us (33%)
  blocking collectives  77.6 us (26%)
  starting transfers between devices  59.5 us (20%)
  matrix products  29.6 us (10%)
  between operations  20.6 us (7%)
  other arithmetic  7.69 us (3%)
  local copies, waits for them, and re-layouts  6.13 us (2%)
    all_to_all x1, starting transfers between devices, per_device(): lax.all_to_all(slot_total, 'wide', split_axis=0, concat_axis=0, tiled=True)  52.4 us
    all_gather x1, waiting for transfers between devices, per_device(): piece = lax.all_gather(normed, 'wide', axis=1, tiled=True)  38.4 us
    all_gather x1, waiting for transfers between devices, per_device(): lax.all_gather(attended_rows, 'wide', axis=0, tiled=True)  36.5 us
    psum x1, blocking collectives, per_device(): squares = lax.psum(jnp.sum(branch * branch, axis=1), 'wide')  31.6 us
    all_gather x1, blocking collectives, per_device(): lax.all_gather(draft_keys, 'wide', axis=0, tiled=True)  23.9 us
    all_gather x1, blocking collectives, per_device(): lax.all_gather(draft_values, 'wide', axis=0, tiled=True)  22.1 us
    all_gather x1, waiting for transfers between devices, per_device(): lax.all_gather(queries, 'wide', axis=0, tiled=True)  9.54 us
    all_to_all x1, waiting for transfers between devices, per_device(): lax.all_to_all(slot_output, 'wide', split_axis=0, concat_axis=0, tiled=True)  9.29 us
  transfers between devices with their start and end apart: 6, of which 5 were waited for; matrix products, arithmetic and copies ran while one was open for 2% of the time, Pallas kernels for 0%

commit v1 on v0

--- a/solution.py
+++ b/solution.py
@@ -6,6 +6,17 @@
 
 very_low = -1e30
 epsilon = 1e-05
+
+
+def turned_line(x, name, dim):
+    n_dev = lax.axis_size(name)
+    route = [(i, (i + 1) % n_dev) for i in range(n_dev)]
+    pieces = [x]
+    for far in range(1, n_dev):
+        pieces = [lax.ppermute(pieces[0], name, route), *pieces]
+    result = jnp.concatenate(pieces, axis=dim)
+    shift = (lax.axis_index(name) + 1) * pieces[-1].shape[dim]
+    return jnp.roll(result, shift, axis=dim)
 
 
 def block_update(state, query_rows, block_keys, block_values, valid, scale):
@@ -162,7 +173,7 @@
     inverse = lax.rsqrt(squares / (columns * devices) + epsilon)
     gain_part = lax.dynamic_slice_in_dim(norm_gain, own_index * columns, columns, 0)
     normed = (branch * inverse[:, None] * gain_part[None, :]).astype(jnp.bfloat16)
-    piece = lax.all_gather(normed, "wide", axis=1, tiled=True)
+    piece = turned_line(normed, "wide", 1)
     gate = jnp.dot(piece, gate_weight, preferred_element_type=jnp.float32)
     upward = jnp.dot(piece, up_weight, preferred_element_type=jnp.float32)
     hidden = (jax.nn.silu(gate) * upward).astype(jnp.bfloat16)

time: 302 us -> 366 us (1.21)
  waiting for transfers between devices: 99.6 us -> 168 us
  matrix products: 29.6 us -> 23.8 us
    ppermute x0 -> x15, waiting for transfers between devices: none -> 106 us  [turned_line(): pieces = [lax.ppermute(pieces[0], name, route), *pieces]]
    all_gather x1 -> x0, waiting for transfers between devices: 38.4 us -> none  [per_device(): piece = lax.all_gather(normed, 'wide', axis=1, tiled=True)]
    dot_general x1, matrix products: 8.32 us -> 3.16 us  [per_device(): upward = jnp.dot(piece, up_weight, preferred_element_type=jnp.float32)]
  transfers between devices with their start and end apart: 6 -> 20, of which waited for: 5 -> 19; matrix products, arithmetic and copies ran while one was open for 2% -> 2% of each run, Pallas kernels for 0% -> 0%
where the time goes in v1:
time: 366 us; the launch traced here: 365 us
  waiting for transfers between devices  168 us (46%)
  blocking collectives  77.5 us (21%)
  starting transfers between devices  59.5 us (16%)
  matrix products  23.8 us (7%)
  between operations  21.2 us (6%)
  local copies, waits for them, and re-layouts  7.97 us (2%)
  other arithmetic  7.19 us (2%)
    ppermute x15, waiting for transfers between devices, turned_line(): pieces = [lax.ppermute(pieces[0], name, route), *pieces]  106 us
    all_to_all x1, starting transfers between devices, per_device(): lax.all_to_all(slot_total, 'wide', split_axis=0, concat_axis=0, tiled=True)  52.3 us
    all_gather x1, waiting for transfers between devices, per_device(): lax.all_gather(attended_rows, 'wide', axis=0, tiled=True)  36.5 us
    psum x1, blocking collectives, per_device(): squares = lax.psum(jnp.sum(branch * branch, axis=1), 'wide')  31.6 us
    all_gather x1, blocking collectives, per_device(): lax.all_gather(draft_keys, 'wide', axis=0, tiled=True)  23.9 us
    all_gather x1, blocking collectives, per_device(): lax.all_gather(draft_values, 'wide', axis=0, tiled=True)  22.1 us
    all_gather x1, waiting for transfers between devices, per_device(): lax.all_gather(queries, 'wide', axis=0, tiled=True)  9.61 us
    all_to_all x1, waiting for transfers between devices, per_device(): lax.all_to_all(slot_output, 'wide', split_axis=0, concat_axis=0, tiled=True)  9.29 us
  transfers between devices with their start and end apart: 20, of which 19 were waited for; matrix products, arithmetic and copies ran while one was open for 2% of the time, Pallas kernels for 0%

profile of v1, /device:TPU:0, one launch (start us, length us, event | category | flops | bytes accessed | tf_op | source)
XLA Modules:
  0.0 365.0 jit_solution(14037851647861395135)
XLA Ops:
  16.7 23.9 %all_gather.13 = bf16[128,512]{1,0:T(8,128)(2,1)S(1)} all-gather(bf16[8,512]{1,0:T(8,128)(2,1)} %param.15), channel_id=1, replica_groups=mesh['grp'=2,'wide'=16] {'wide'}, dimensions={0}, use_global_device_ids=true | all-gather | bytes 139264 | tf_op jit(solution)/shard_map/all_gather | solution.py:109
  41.3 9.6 %all-gather.3.cloned.1.call-done = bf16[128,4096]{1,0:T(8,128)(2,1)} async-done(((bf16[8,4096]{1,0:T(8,128)(2,1)}), bf16[128,4096]{1,0:T(8,128)(2,1)}) %all-gather.3.cloned.1.call-update) | async-done | bytes 1048592 | tf_op jit(solution)/shard_map/all_gather | solution.py:108
  52.5 11.5 %while.15 = (s32[]{:T(128)}, f32[64,8]{0,1:T(8,128)S(1)}, f32[64,8]{0,1:T(8,128)S(1)}, f32[64,8,128]{2,1,0:T(8,128)S(1)}, s32[]{:T(128)}, /*index=5*/s32[]{:T(12...) while((s32[]{:T(128)}, f32[64,8]{0,1:T(8,128)S(1)}, ...), condition=%wide.region_8.9_spmd.clone, body=%wide.region_5.8_spmd.clone.sunk | while | flops 136185856 | bytes 4099771 | solution.py:62
  65.5 52.3 %all-to-all-start.2 = ((f32[16,8,8]{1,2,0:T(8,128)}), f32[16,8,8]{1,2,0:T(8,128)S(1)}, u32[]{:S(2)}, u32[]{:S(2)}) async-start(f32[16,8,8]{1,2,0:T(8,128)} %copy.68), calls=%async_computation.2 | async-start | bytes 131072 | tf_op jit(solution)/shard_map/all_to_all | solution.py:148
  117.8 22.1 %all_gather.14 = bf16[128,512]{1,0:T(8,128)(2,1)S(1)} all-gather(bf16[8,512]{1,0:T(8,128)(2,1)S(1)} %copy-done.1), channel_id=1, replica_groups=mesh['grp'=2,'wide'=16] {'wide'}, dimensions={0}, use_global_device_ids=true | all-gather | bytes 139264 | tf_op jit(solution)/shard_map/all_gather | solution.py:110
  155.6 9.3 %all-to-all-done = bf16[16,8,8,128]{3,2,1,0:T(8,128)(2,1)S(1)} async-done(((bf16[16,8,8,128]{3,2,1,0:T(8,128)(2,1)}), bf16[16,8,8,128]{3,2,1,0:T(8,128)(2,1)S(1)}, u32[]{:S(2)}, u32[]{:S(2)}) %all-to-all-start) | async-done | bytes 262176 | tf_op jit(solution)/shard_map/all_to_all | solution.py:150
  167.0 36.5 %all-gather.5.cloned.1.call-done = bf16[128,4096]{1,0:T(8,128)(2,1)} async-done(((bf16[8,4096]{1,0:T(8,128)(2,1)}), bf16[128,4096]{1,0:T(8,128)(2,1)}) %all-gather.5.cloned.1.call-update) | async-done | bytes 1048592 | tf_op jit(solution)/shard_map/all_gather | solution.py:165
  206.9 31.6 %psum.7 = f32[128]{0:T(128)S(1)} all-reduce(f32[128]{0:T(128)S(1)} %fusion.24), channel_id=1, replica_groups=mesh['grp'=2,'wide'=16] {'wide'}, use_global_device_ids=true, to_apply=%region_15.16 | all-reduce | flops 128 | bytes 1024 | tf_op jit(solution)/shard_map/psum | solution.py:172
  238.6 7.1 %collective-permute-done = bf16[128,512]{1,0:T(8,128)(2,1)S(1)} collective-permute-done((bf16[128,512]{1,0:T(8,128)(2,1)S(1)}, bf16[128,512]{1,0:T(8,128)(2,1)S(1)}, u32[]{:S(2)}, u32[]{:S(2)}) %collective-permute-start) | collective-permute-done | bytes 131104 | tf_op jit(solution)/shard_map/ppermute | solution.py:16
  245.7 7.1 %collective-permute-done.1 = bf16[128,512]{1,0:T(8,128)(2,1)S(1)} collective-permute-done((bf16[128,512]{1,0:T(8,128)(2,1)S(1)}, bf16[128,512]{1,0:T(8,128)(2,1)S(1)}, u32[]{:S(2)}, u32[]{:S(2)}) %collective-permute-start.1) | collective-permute-done | bytes 131104 | tf_op jit(solution)/shard_map/ppermute | solution.py:16
  252.8 7.1 %collective-permute-done.2 = bf16[128,512]{1,0:T(8,128)(2,1)S(1)} collective-permute-done((bf16[128,512]{1,0:T(8,128)(2,1)S(1)}, bf16[128,512]{1,0:T(8,128)(2,1)S(1)}, u32[]{:S(2)}, u32[]{:S(2)}) %collective-permute-start.2) | collective-permute-done | bytes 131104 | tf_op jit(solution)/shard_map/ppermute | solution.py:16
  259.9 7.1 %collective-permute-done.3 = bf16[128,512]{1,0:T(8,128)(2,1)S(1)} collective-permute-done((bf16[128,512]{1,0:T(8,128)(2,1)S(1)}, bf16[128,512]{1,0:T(8,128)(2,1)S(1)}, u32[]{:S(2)}, u32[]{:S(2)}) %collective-permute-start.3) | collective-permute-done | bytes 131104 | tf_op jit(solution)/shard_map/ppermute | solution.py:16
  267.0 7.1 %collective-permute-done.4 = bf16[128,512]{1,0:T(8,128)(2,1)S(1)} collective-permute-done((bf16[128,512]{1,0:T(8,128)(2,1)S(1)}, bf16[128,512]{1,0:T(8,128)(2,1)S(1)}, u32[]{:S(2)}, u32[]{:S(2)}) %collective-permute-start.4) | collective-permute-done | bytes 131104 | tf_op jit(solution)/shard_map/ppermute | solution.py:16
  274.1 7.1 %collective-permute-done.5 = bf16[128,512]{1,0:T(8,128)(2,1)S(1)} collective-permute-done((bf16[128,512]{1,0:T(8,128)(2,1)S(1)}, bf16[128,512]{1,0:T(8,128)(2,1)S(1)}, u32[]{:S(2)}, u32[]{:S(2)}) %collective-permute-start.5) | collective-permute-done | bytes 131104 | tf_op jit(solution)/shard_map/ppermute | solution.py:16
  281.2 7.1 %collective-permute-done.6 = bf16[128,512]{1,0:T(8,128)(2,1)S(1)} collective-permute-done((bf16[128,512]{1,0:T(8,128)(2,1)S(1)}, bf16[128,512]{1,0:T(8,128)(2,1)S(1)}, u32[]{:S(2)}, u32[]{:S(2)}) %collective-permute-start.6) | collective-permute-done | bytes 131104 | tf_op jit(solution)/shard_map/ppermute | solution.py:16
  288.3 7.1 %collective-permute-done.7 = bf16[128,512]{1,0:T(8,128)(2,1)S(1)} collective-permute-done((bf16[128,512]{1,0:T(8,128)(2,1)S(1)}, bf16[128,512]{1,0:T(8,128)(2,1)S(1)}, u32[]{:S(2)}, u32[]{:S(2)}) %collective-permute-start.7) | collective-permute-done | bytes 131104 | tf_op jit(solution)/shard_map/ppermute | solution.py:16
  295.4 7.1 %collective-permute-done.8 = bf16[128,512]{1,0:T(8,128)(2,1)S(1)} collective-permute-done((bf16[128,512]{1,0:T(8,128)(2,1)S(1)}, bf16[128,512]{1,0:T(8,128)(2,1)S(1)}, u32[]{:S(2)}, u32[]{:S(2)}) %collective-permute-start.8) | collective-permute-done | bytes 131104 | tf_op jit(solution)/shard_map/ppermute | solution.py:16
  302.4 7.1 %collective-permute-done.9 = bf16[128,512]{1,0:T(8,128)(2,1)S(1)} collective-permute-done((bf16[128,512]{1,0:T(8,128)(2,1)S(1)}, bf16[128,512]{1,0:T(8,128)(2,1)S(1)}, u32[]{:S(2)}, u32[]{:S(2)}) %collective-permute-start.9) | collective-permute-done | bytes 131104 | tf_op jit(solution)/shard_map/ppermute | solution.py:16
  309.5 7.1 %collective-permute-done.10 = bf16[128,512]{1,0:T(8,128)(2,1)S(1)} collective-permute-done((bf16[128,512]{1,0:T(8,128)(2,1)S(1)}, bf16[128,512]{1,0:T(8,128)(2,1)S(1)}, u32[]{:S(2)}, u32[]{:S(2)}) %collective-permute-start.10) | collective-permute-done | bytes 131104 | tf_op jit(solution)/shard_map/ppermute | solution.py:16
  316.6 7.1 %collective-permute-done.11 = bf16[128,512]{1,0:T(8,128)(2,1)S(1)} collective-permute-done((bf16[128,512]{1,0:T(8,128)(2,1)S(1)}, bf16[128,512]{1,0:T(8,128)(2,1)S(1)}, u32[]{:S(2)}, u32[]{:S(2)}) %collective-permute-start.11) | collective-permute-done | bytes 131104 | tf_op jit(solution)/shard_map/ppermute | solution.py:16
  323.7 7.1 %collective-permute-done.12 = bf16[128,512]{1,0:T(8,128)(2,1)S(1)} collective-permute-done((bf16[128,512]{1,0:T(8,128)(2,1)S(1)}, bf16[128,512]{1,0:T(8,128)(2,1)S(1)}, u32[]{:S(2)}, u32[]{:S(2)}) %collective-permute-start.12) | collective-permute-done | bytes 131104 | tf_op jit(solution)/shard_map/ppermute | solution.py:16
  330.8 7.1 %collective-permute-done.13 = bf16[128,512]{1,0:T(8,128)(2,1)S(1)} collective-permute-done((bf16[128,512]{1,0:T(8,128)(2,1)S(1)}, bf16[128,512]{1,0:T(8,128)(2,1)S(1)}, u32[]{:S(2)}, u32[]{:S(2)}) %collective-permute-start.13) | collective-permute-done | bytes 131104 | tf_op jit(solution)/shard_map/ppermute | solution.py:16
  337.9 7.1 %collective-permute-done.14 = bf16[128,512]{1,0:T(8,128)(2,1)S(1)} collective-permute-done((bf16[128,512]{1,0:T(8,128)(2,1)S(1)}, bf16[128,512]{1,0:T(8,128)(2,1)S(1)}, u32[]{:S(2)}, u32[]{:S(2)}) %collective-permute-start.14) | collective-permute-done | bytes 131104 | tf_op jit(solution)/shard_map/ppermute | solution.py:16
  345.8 7.7 %fusion.16 = f32[128,896]{1,0:T(8,128)S(1)} fusion(bf16[8192,896]{1,0:T(8,128)(2,1)} %param.24, bf16[128,16384]{1,0:T(8,128)(2,1)S(1)} %constant_dynamic-update-slice_fusion, s32[]{:T(128)S(6)} %select_n.115), kind=kOutput, calls=%fused_computation.21 | convolution fusion | flops 1879048192 | bytes 17235972 | tf_op jit(solution)/shard_map/dot_general | solution.py:177
  (135 shorter events, 44.4 us)
Async XLA Ops:
  7.2 43.8 %all-gather.3.cloned.1.call-start = ((), (), s32[]{:S(2)}) async-start(), calls=%async_computation.3 | async-start | bytes 1114112 | tf_op jit(solution)/shard_map/all_gather | solution.py:108
  52.5 65.3 %copy-start.1 = (bf16[8,512]{1,0:T(8,128)(2,1)S(1)}, bf16[8,512]{1,0:T(8,128)(2,1)}, u32[]{:S(2)}) copy-start(bf16[8,512]{1,0:T(8,128)(2,1)} %param.16) | copy-start | bytes 24580
  65.5 75.6 %all-to-all-start.2 = ((f32[16,8,8]{1,2,0:T(8,128)}), f32[16,8,8]{1,2,0:T(8,128)S(1)}, u32[]{:S(2)}, u32[]{:S(2)}) async-start(f32[16,8,8]{1,2,0:T(8,128)} %copy.68), calls=%async_computation.2 | async-start | bytes 131072 | tf_op jit(solution)/shard_map/all_to_all | solution.py:148
  141.0 10.4 %all-to-all-start.1 = ((f32[16,8,8]{1,2,0:T(8,128)}), f32[16,8,8]{1,2,0:T(8,128)S(1)}, u32[]{:S(2)}, u32[]{:S(2)}) async-start(f32[16,8,8]{1,2,0:T(8,128)} %copy.66), calls=%async_computation.1 | async-start | bytes 131072 | tf_op jit(solution)/shard_map/all_to_all | solution.py:147
  151.4 13.5 %all-to-all-start = ((bf16[16,8,8,128]{3,2,1,0:T(8,128)(2,1)}), bf16[16,8,8,128]{3,2,1,0:T(8,128)(2,1)S(1)}, u32[]{:S(2)}, u32[]{:S(2)}) async-start(bf16[16,8,8,128]{3,2,1,0:T(8,128)(2,1)} %bitcast.3), calls=%async_computation | async-start | bytes 524288 | tf_op jit(solution)/shard_map/all_to_all | solution.py:150
  155.0 48.5 %all-gather.5.cloned.1.call-start = ((), (), s32[]{:S(2)}) async-start(), calls=%async_computation.4 | async-start | bytes 1114112 | tf_op jit(solution)/shard_map/all_gather | solution.py:165
  206.7 138.9 %copy-start = (bf16[128,512]{1,0:T(8,128)(2,1)}, bf16[128,512]{1,0:T(8,128)(2,1)S(1)}, u32[]{:S(2)}) copy-start(bf16[128,512]{1,0:T(8,128)(2,1)S(1)} %convolution_convert_fusion) | copy-start | bytes 393220
  238.6 7.1 %collective-permute-start = (bf16[128,512]{1,0:T(8,128)(2,1)S(1)}, bf16[128,512]{1,0:T(8,128)(2,1)S(1)}, u32[]{:S(2)}, u32[]{:S(2)}) collective-permute-start(bf16[128,512]{1,0:T(8,128)(2,1)S(1)} %fusion.26), channel_id=1, source_target_pairs={{0,1},{1,2},{2,3},{3,4},{4,5},{5,6},{6,7},{7,8},{8,9},{9,10},{10,1... | collective-permute-start | bytes 393224 | tf_op jit(solution)/shard_map/ppermute | solution.py:16
  245.7 7.1 %collective-permute-start.1 = (bf16[128,512]{1,0:T(8,128)(2,1)S(1)}, bf16[128,512]{1,0:T(8,128)(2,1)S(1)}, u32[]{:S(2)}, u32[]{:S(2)}) collective-permute-start(bf16[128,512]{1,0:T(8,128)(2,1)S(1)} %collective-permute-done), channel_id=1, source_target_pairs={{0,1},{1,2},{2,3},{3,4},{4,5},{5,6},{6,7},{7,8},{8,9},{9,10},{10,1... | collective-permute-start | bytes 393224 | tf_op jit(solution)/shard_map/ppermute | solution.py:16
  252.8 7.1 %collective-permute-start.2 = (bf16[128,512]{1,0:T(8,128)(2,1)S(1)}, bf16[128,512]{1,0:T(8,128)(2,1)S(1)}, u32[]{:S(2)}, u32[]{:S(2)}) collective-permute-start(bf16[128,512]{1,0:T(8,128)(2,1)S(1)} %collective-permute-done.1), channel_id=1, source_target_pairs={{0,1},{1,2},{2,3},{3,4},{4,5},{5,6},{6,7},{7,8},{8,9},{9,10},{10,1... | collective-permute-start | bytes 393224 | tf_op jit(solution)/shard_map/ppermute | solution.py:16
  259.9 7.1 %collective-permute-start.3 = (bf16[128,512]{1,0:T(8,128)(2,1)S(1)}, bf16[128,512]{1,0:T(8,128)(2,1)S(1)}, u32[]{:S(2)}, u32[]{:S(2)}) collective-permute-start(bf16[128,512]{1,0:T(8,128)(2,1)S(1)} %collective-permute-done.2), channel_id=1, source_target_pairs={{0,1},{1,2},{2,3},{3,4},{4,5},{5,6},{6,7},{7,8},{8,9},{9,10},{10,1... | collective-permute-start | bytes 393224 | tf_op jit(solution)/shard_map/ppermute | solution.py:16
  267.0 7.1 %collective-permute-start.4 = (bf16[128,512]{1,0:T(8,128)(2,1)S(1)}, bf16[128,512]{1,0:T(8,128)(2,1)S(1)}, u32[]{:S(2)}, u32[]{:S(2)}) collective-permute-start(bf16[128,512]{1,0:T(8,128)(2,1)S(1)} %collective-permute-done.3), channel_id=1, source_target_pairs={{0,1},{1,2},{2,3},{3,4},{4,5},{5,6},{6,7},{7,8},{8,9},{9,10},{10,1... | collective-permute-start | bytes 393224 | tf_op jit(solution)/shard_map/ppermute | solution.py:16
  274.1 7.1 %collective-permute-start.5 = (bf16[128,512]{1,0:T(8,128)(2,1)S(1)}, bf16[128,512]{1,0:T(8,128)(2,1)S(1)}, u32[]{:S(2)}, u32[]{:S(2)}) collective-permute-start(bf16[128,512]{1,0:T(8,128)(2,1)S(1)} %collective-permute-done.4), channel_id=1, source_target_pairs={{0,1},{1,2},{2,3},{3,4},{4,5},{5,6},{6,7},{7,8},{8,9},{9,10},{10,1... | collective-permute-start | bytes 393224 | tf_op jit(solution)/shard_map/ppermute | solution.py:16
  281.2 7.1 %collective-permute-start.6 = (bf16[128,512]{1,0:T(8,128)(2,1)S(1)}, bf16[128,512]{1,0:T(8,128)(2,1)S(1)}, u32[]{:S(2)}, u32[]{:S(2)}) collective-permute-start(bf16[128,512]{1,0:T(8,128)(2,1)S(1)} %collective-permute-done.5), channel_id=1, source_target_pairs={{0,1},{1,2},{2,3},{3,4},{4,5},{5,6},{6,7},{7,8},{8,9},{9,10},{10,1... | collective-permute-start | bytes 393224 | tf_op jit(solution)/shard_map/ppermute | solution.py:16
  288.3 7.1 %collective-permute-start.7 = (bf16[128,512]{1,0:T(8,128)(2,1)S(1)}, bf16[128,512]{1,0:T(8,128)(2,1)S(1)}, u32[]{:S(2)}, u32[]{:S(2)}) collective-permute-start(bf16[128,512]{1,0:T(8,128)(2,1)S(1)} %collective-permute-done.6), channel_id=1, source_target_pairs={{0,1},{1,2},{2,3},{3,4},{4,5},{5,6},{6,7},{7,8},{8,9},{9,10},{10,1... | collective-permute-start | bytes 393224 | tf_op jit(solution)/shard_map/ppermute | solution.py:16
  295.3 7.1 %collective-permute-start.8 = (bf16[128,512]{1,0:T(8,128)(2,1)S(1)}, bf16[128,512]{1,0:T(8,128)(2,1)S(1)}, u32[]{:S(2)}, u32[]{:S(2)}) collective-permute-start(bf16[128,512]{1,0:T(8,128)(2,1)S(1)} %collective-permute-done.7), channel_id=1, source_target_pairs={{0,1},{1,2},{2,3},{3,4},{4,5},{5,6},{6,7},{7,8},{8,9},{9,10},{10,1... | collective-permute-start | bytes 393224 | tf_op jit(solution)/shard_map/ppermute | solution.py:16
  302.4 7.1 %collective-permute-start.9 = (bf16[128,512]{1,0:T(8,128)(2,1)S(1)}, bf16[128,512]{1,0:T(8,128)(2,1)S(1)}, u32[]{:S(2)}, u32[]{:S(2)}) collective-permute-start(bf16[128,512]{1,0:T(8,128)(2,1)S(1)} %collective-permute-done.8), channel_id=1, source_target_pairs={{0,1},{1,2},{2,3},{3,4},{4,5},{5,6},{6,7},{7,8},{8,9},{9,10},{10,1... | collective-permute-start | bytes 393224 | tf_op jit(solution)/shard_map/ppermute | solution.py:16
  309.5 7.1 %collective-permute-start.10 = (bf16[128,512]{1,0:T(8,128)(2,1)S(1)}, bf16[128,512]{1,0:T(8,128)(2,1)S(1)}, u32[]{:S(2)}, u32[]{:S(2)}) collective-permute-start(bf16[128,512]{1,0:T(8,128)(2,1)S(1)} %collective-permute-done.9), channel_id=1, source_target_pairs={{0,1},{1,2},{2,3},{3,4},{4,5},{5,6},{6,7},{7,8},{8,9},{9,10},{10,1... | collective-permute-start | bytes 393224 | tf_op jit(solution)/shard_map/ppermute | solution.py:16
  316.6 7.1 %collective-permute-start.11 = (bf16[128,512]{1,0:T(8,128)(2,1)S(1)}, bf16[128,512]{1,0:T(8,128)(2,1)S(1)}, u32[]{:S(2)}, u32[]{:S(2)}) collective-permute-start(bf16[128,512]{1,0:T(8,128)(2,1)S(1)} %collective-permute-done.10), channel_id=1, source_target_pairs={{0,1},{1,2},{2,3},{3,4},{4,5},{5,6},{6,7},{7,8},{8,9},{9,10},{10,1... | collective-permute-start | bytes 393224 | tf_op jit(solution)/shard_map/ppermute | solution.py:16
  323.7 7.1 %collective-permute-start.12 = (bf16[128,512]{1,0:T(8,128)(2,1)S(1)}, bf16[128,512]{1,0:T(8,128)(2,1)S(1)}, u32[]{:S(2)}, u32[]{:S(2)}) collective-permute-start(bf16[128,512]{1,0:T(8,128)(2,1)S(1)} %collective-permute-done.11), channel_id=1, source_target_pairs={{0,1},{1,2},{2,3},{3,4},{4,5},{5,6},{6,7},{7,8},{8,9},{9,10},{10,1... | collective-permute-start | bytes 393224 | tf_op jit(solution)/shard_map/ppermute | solution.py:16
  330.8 7.1 %collective-permute-start.13 = (bf16[128,512]{1,0:T(8,128)(2,1)S(1)}, bf16[128,512]{1,0:T(8,128)(2,1)S(1)}, u32[]{:S(2)}, u32[]{:S(2)}) collective-permute-start(bf16[128,512]{1,0:T(8,128)(2,1)S(1)} %collective-permute-done.12), channel_id=1, source_target_pairs={{0,1},{1,2},{2,3},{3,4},{4,5},{5,6},{6,7},{7,8},{8,9},{9,10},{10,1... | collective-permute-start | bytes 393224 | tf_op jit(solution)/shard_map/ppermute | solution.py:16
  337.9 7.1 %collective-permute-start.14 = (bf16[128,512]{1,0:T(8,128)(2,1)S(1)}, bf16[128,512]{1,0:T(8,128)(2,1)S(1)}, u32[]{:S(2)}, u32[]{:S(2)}) collective-permute-start(bf16[128,512]{1,0:T(8,128)(2,1)S(1)} %collective-permute-done.13), channel_id=1, source_target_pairs={{0,1},{1,2},{2,3},{3,4},{4,5},{5,6},{6,7},{7,8},{8,9},{9,10},{10,1... | collective-permute-start | bytes 393224 | tf_op jit(solution)/shard_map/ppermute | solution.py:16
  345.8 8.6 %slice-start.2 = ((s8[14680064]{0:T(1024)(128)(4,1)}), s8[4194304]{0:T(1024)(128)(4,1)S(1)}, s32[]{:S(2)}) async-start(s8[14680064]{0:T(1024)(128)(4,1)} %bitcast.62), calls=%async_computation.7 | async-start | bytes 8388608
  345.8 9.2 %slice-start.3 = ((s8[14680064]{0:T(1024)(128)(4,1)}), s8[2097152]{0:T(1024)(128)(4,1)S(1)}, s32[]{:S(2)}) async-start(s8[14680064]{0:T(1024)(128)(4,1)} %bitcast.62), calls=%async_computation.8 | async-start | bytes 4194304
  (2 other events, 15.7 us)
Sparse Core Ops, SparseCore 0:
  10.1 40.7 all-gather.2
  166.3 37.1 all-gather.4
